TPU v7x, 32 devices: a whole 2x2x4 slice. The times are simulated.
32 devices in a mesh: fsdp: 8 (over z, y), tp: 4 (over x, core).
Axes of the slice: x: 2, y: 2, z: 4, core: 2. Of those that a mesh axis runs over, the one named last changes fastest.
Arguments:
- states: bfloat16 [8, 8, 32, 4096], P('fsdp', None, None, 'tp'), may hold values from -40 to 40
- dest: int32 [8, 8], P('fsdp'), may hold values from 0 to 7, each once within a row
- lengths: int32 [8, 8], P('fsdp'), may hold values from 1 to 32, 160 in all within a row
- strata: int32 [8, 8, 1], P('fsdp'), may hold values from 0 to 7
- ffn_gain: float32 [4096], replicated, may hold values from 0.1 to 1.9
- gate_weight: bfloat16 [4096, 7168], P('fsdp', 'tp'), may hold values from -0.0703125 to 0.0703125
- up_weight: bfloat16 [4096, 7168], P('fsdp', 'tp'), may hold values from -0.1 to 0.1
- down_weight: bfloat16 [7168, 4096], P('tp', 'fsdp'), may hold values from -0.058238643 to 0.058238643
- final_gain: float32 [4096], replicated, may hold values from 0.1 to 1.9
- value_weight: float32 [4096], replicated, may hold values from -0.09375 to 0.09375
Outputs:
- rewards: float32 [8, 8], P('fsdp')
- stratum_means: float32 [8], replicated
Inputs may be any that keep to these rules, and one draw needn't show every extreme that they name: Each row of dest is a permutation: every source group sends exactly one response to every scoring group. Each source group's lengths sum to 160. `strata`: every stratum holds at least one response.
All inputs are finite; a program needn't handle non-finite values.
Results may differ from a plain program's by a relative error of at most 0.004.
Values may be sent and summed in bfloat16 or wider, within the bound.
A program may use at most 128 MiB of HBM per device.

v0:
```python
import jax
import jax.numpy as jnp
from jax import lax
from jax.sharding import PartitionSpec as P

S = 8


epsilon = 1e-05


def body(
    states,
    dest,
    lengths,
    strata,
    ffn_gain,
    gate_weight,
    up_weight,
    down_weight,
    final_gain,
    value_weight,
):
    groups = dest.shape[1]
    length = states.shape[2]
    slots = jnp.arange(groups, dtype=jnp.int32)
    picker = (dest[0][None, :] == slots[:, None]).astype(jnp.int32)
    source_slot = jnp.sum(picker * slots[None, :], axis=1)
    outgoing = jnp.take(states[0], source_slot, axis=0)
    out_len = jnp.take(lengths[0], source_slot, axis=0)
    out_str = jnp.take(strata[0, :, 0], source_slot, axis=0)
    received, recv_len, recv_str = (
        lax.all_to_all(outgoing, "fsdp", split_axis=0, concat_axis=0, tiled=True),
        lax.all_to_all(out_len, "fsdp", split_axis=0, concat_axis=0, tiled=True),
        lax.all_to_all(out_str, "fsdp", split_axis=0, concat_axis=0, tiled=True),
    )
    gathered = lax.all_gather(received, "tp", axis=2, tiled=True)
    feature_width = gathered.shape[2]
    token_count = groups * length
    widened = gathered.reshape(token_count, feature_width).astype(jnp.float32)
    normed = (
        widened
        * lax.rsqrt(jnp.mean(widened * widened, axis=1, keepdims=True) + epsilon)
        * ffn_gain[None, :]
    ).astype(jnp.bfloat16)
    gate_full, up_full, down_full = (
        lax.all_gather(gate_weight, "fsdp", axis=0, tiled=True),
        lax.all_gather(up_weight, "fsdp", axis=0, tiled=True),
        lax.all_gather(down_weight, "fsdp", axis=1, tiled=True),
    )
    gate = jnp.dot(normed, gate_full, preferred_element_type=jnp.float32)
    up_part = jnp.dot(normed, up_full, preferred_element_type=jnp.float32)
    hidden = (jax.nn.silu(gate) * up_part).astype(jnp.bfloat16)
    partial_value = jnp.dot(hidden, down_full, preferred_element_type=jnp.float32)
    head_scale = final_gain * value_weight
    total = lax.psum(partial_value.astype(jnp.bfloat16), "tp").astype(jnp.float32)
    mixed = widened + total
    product = jnp.sum(mixed * head_scale[None, :], axis=1)
    value = product * lax.rsqrt(jnp.mean(mixed * mixed, axis=1) + epsilon)
    value = value.reshape(groups, length)
    positions = jnp.arange(length, dtype=jnp.int32)
    live_mask = (positions[None, :] < recv_len[:, None]).astype(jnp.float32)
    reward = jnp.sum(value * live_mask, axis=1) / recv_len.astype(jnp.float32)
    strata_ids = jnp.arange(S, dtype=jnp.int32)
    onehot = (recv_str[:, None] == strata_ids[None, :]).astype(jnp.float32)
    sums = jnp.sum(reward[:, None] * onehot, axis=0)
    counts = jnp.sum(onehot, axis=0)
    sums, counts = lax.psum((sums, counts), "fsdp")
    return (reward.reshape(1, groups), sums / counts)


def solution(mesh):
    return jax.shard_map(
        body,
        mesh=mesh,
        in_specs=(
            P("fsdp", None, None, "tp"),
            P("fsdp", None),
            P("fsdp", None),
            P("fsdp", None, None),
            P(),
            P("fsdp", "tp"),
            P("fsdp", "tp"),
            P("tp", "fsdp"),
            P(),
            P(),
        ),
        out_specs=(P("fsdp", None), P()),
        check_vma=False,
    )
```

profile of v0, /device:TPU:0, one launch (start us, length us, event | category | flops | bytes accessed | tf_op | source)
XLA Modules:
  0.0 764.5 jit_solution(11980279169275734645)
XLA Ops:
  7.2 0.0 copy-start
  7.2 0.0 all-gather.5.cloned.1.call-start
  7.2 0.8 select_reduce_fusion.2
  8.1 1.3 gather_fusion.2
  9.4 0.0 copy-done
  9.4 0.6 gather_fusion
  10.0 0.1 broadcast_select_fusion
  10.1 21.7 %all_to_all.23 = bf16[8,32,1024]{2,1,0:T(8,128)(2,1)} all-to-all(bf16[8,32,1024]{2,1,0:T(8,128)(2,1)S(1)} %broadcast_select_fusion), channel_id=1, replica_groups=mesh['fsdp'=8,'tp'=4] {'fsdp'}, dimensions={0} | all-to-all | bytes 1048576 | tf_op jit(solution)/shard_map/all_to_all | solution.py:33
  31.8 0.0 all-gather.5.cloned.1.call-update
  31.9 0.0 all-gather.7.cloned.1.call-start
  31.9 0.7 all-gather.7.cloned.1.call-update
  32.6 0.0 all-gather.11.cloned.1.call-start
  32.7 0.7 all-gather.11.cloned.1.call-update
  33.3 0.0 copy-start.3
  33.4 0.0 all-gather.9.cloned.1.call-start
  33.4 0.5 all-gather.9.cloned.1.call-update
  33.9 0.0 all-reduce.3.cloned.1.call-start
  34.0 19.6 %all-gather.5.cloned.1.call-done = bf16[8,32,4096]{2,1,0:T(8,128)(2,1)} async-done(((bf16[8,32,1024]{2,1,0:T(8,128)(2,1)}), bf16[8,32,4096]{2,1,0:T(8,128)(2,1)}) %all-gather.5.cloned.1.call-update) | async-done | bytes 2097168 | tf_op jit(solution)/shard_map/all_gather | solution.py:37
  53.6 2.2 fusion
  55.8 0.1 rsqrt.17
  55.9 0.0 copy-done.3
  55.9 0.0 copy-done.2
  55.9 1.9 fusion.2
  57.9 200.0 %all-gather.7.cloned.1.call-done = bf16[4096,1792]{1,0:T(8,128)(2,1)} async-done(((bf16[512,1792]{1,0:T(8,128)(2,1)}), bf16[4096,1792]{1,0:T(8,128)(2,1)}) %all-gather.7.cloned.1.call-update) | async-done | bytes 14680080 | tf_op jit(solution)/shard_map/all_gather | solution.py:47
  257.8 11.0 %fusion.6 = f32[256,1792]{1,0:T(8,128)} fusion(bf16[256,4096]{1,0:T(8,128)(2,1)} %fusion.2, bf16[4096,1792]{1,0:T(8,128)(2,1)} %all-gather.7.cloned.1.call-done), kind=kOutput, calls=%fused_computation.36 | convolution fusion | flops 3758096384 | bytes 18612224 | tf_op jit(solution)/shard_map/dot_general | solution.py:51
  268.9 191.5 %all-gather.11.cloned.1.call-done = bf16[1792,4096]{1,0:T(8,128)(2,1)} async-done(((bf16[1792,512]{1,0:T(8,128)(2,1)}), bf16[1792,4096]{1,0:T(8,128)(2,1)}) %all-gather.11.cloned.1.call-update) | async-done | bytes 14680080 | tf_op jit(solution)/shard_map/all_gather | solution.py:49
  460.4 202.3 %all-gather.9.cloned.1.call-done = bf16[4096,1792]{1,0:T(8,128)(2,1)} async-done(((bf16[512,1792]{1,0:T(8,128)(2,1)}), bf16[4096,1792]{1,0:T(8,128)(2,1)}) %all-gather.9.cloned.1.call-update) | async-done | bytes 14680080 | tf_op jit(solution)/shard_map/all_gather | solution.py:48
  662.6 20.2 %convolution_convert_fusion = bf16[256,4096]{1,0:T(8,128)(2,1)} fusion(bf16[1792,4096]{1,0:T(8,128)(2,1)} %all-gather.11.cloned.1.call-done, bf16[256,4096]{1,0:T(8,128)(2,1)} %fusion.2, bf16[4096,1792]{1,0:T(8,128)(2,1)} %all-gather.9.cloned.1.call-done, f32[256,1792]{1,0:T(8,128)} %fusion.6), kind=kOutput, calls=%fused_computation.3 | convolution fusion | flops 7519993856 | bytes 35389440 | tf_op jit(solution)/shard_map/dot_general | solution.py:54
  682.8 0.0 all-reduce.3.cloned.1.call-update
  682.8 0.6 copy-done.1
  683.4 0.6 gather_fusion.1
  684.1 0.7 copy.16
  684.8 3.3 all-to-all-start
  688.0 0.7 copy.17
  688.7 5.7 all-to-all-done
  694.4 3.3 all-to-all-start.2
  697.7 0.2 reduce.1
  698.0 6.2 all-to-all-done.2
  704.1 0.2 reduce.3
  704.4 0.1 convert_reduce_fusion.1
  704.5 28.0 %all-reduce.3.cloned.1.call-done = bf16[256,4096]{1,0:T(8,128)(2,1)} async-done(((bf16[256,4096]{1,0:T(8,128)(2,1)}), bf16[256,4096]{1,0:T(8,128)(2,1)}) %all-reduce.3.cloned.1.call-update) | async-done | bytes 2097168 | tf_op jit(solution)/shard_map/psum | solution.py:56
  732.5 2.7 multiply_reduce_fusion
  735.2 0.1 mul.83
  735.3 0.2 select_reduce_fusion.1
  735.5 0.5 bitcast_divide_fusion
  736.0 0.1 convert_reduce_fusion
  736.1 21.4 %all-reduce = (f32[8]{0:T(128)S(1)}, f32[8]{0:T(128)S(1)}) all-reduce(f32[8]{0:T(128)S(1)} %get-tuple-element.6, f32[8]{0:T(128)S(1)} %get-tuple-element.5), channel_id=1, replica_groups=mesh['fsdp'=8,'tp'=4] {'fsdp'}, use_global_device_ids=true, to_apply=%region_7.9 | all-reduce | flops 16 | bytes 128 | tf_op jit(solution)/shard_map/psum | solution.py:68
  757.5 0.5 div.42
  (16 shorter events, 0.1 us)
Async XLA Ops:
  7.2 2.2 copy-start
  7.2 46.4 %all-gather.5.cloned.1.call-start = ((), (), s32[]{:S(2)}) async-start(), calls=%async_computation.3 | async-start | bytes 2621440 | tf_op jit(solution)/shard_map/all_gather | solution.py:37
  31.9 226.0 %all-gather.7.cloned.1.call-start = ((), (), s32[]{:S(2)}) async-start(), calls=%async_computation.4 | async-start | bytes 16515072 | tf_op jit(solution)/shard_map/all_gather | solution.py:47
  32.6 427.7 %all-gather.11.cloned.1.call-start = ((), (), s32[]{:S(2)}) async-start(), calls=%async_computation.6 | async-start | bytes 16515072 | tf_op jit(solution)/shard_map/all_gather | solution.py:49
  33.3 22.6 %copy-start.3 = (f32[4096]{0:T(1024)S(1)}, f32[4096]{0:T(1024)}, u32[]{:S(2)}) copy-start(f32[4096]{0:T(1024)} %param.16) | copy-start | bytes 49156
  33.4 629.3 %all-gather.9.cloned.1.call-start = ((), (), s32[]{:S(2)}) async-start(), calls=%async_computation.5 | async-start | bytes 16515072 | tf_op jit(solution)/shard_map/all_gather | solution.py:48
  33.9 698.6 %all-reduce.3.cloned.1.call-start = ((), (), s32[]{:S(2)}) async-start(), calls=%async_computation.7 | async-start | bytes 4194304 | tf_op jit(solution)/shard_map/psum | solution.py:56
  53.6 2.3 copy-start.2
  682.8 0.7 copy-start.1
  682.8 5.9 copy-start.4
  682.8 5.9 copy-start.5
  684.8 9.7 %all-to-all-start = ((s32[8,1,1]{2,1,0:T(1,128)}), s32[8,1,1]{2,1,0:T(1,128)S(1)}, u32[]{:S(2)}, u32[]{:S(2)}) async-start(s32[8,1,1]{2,1,0:T(1,128)} %copy.16), calls=%async_computation | async-start | bytes 8192 | tf_op jit(solution)/shard_map/all_to_all | solution.py:34
  694.4 9.7 %all-to-all-start.2 = ((s32[8,1,1]{2,1,0:T(1,128)}), s32[8,1,1]{2,1,0:T(1,128)S(1)}, u32[]{:S(2)}, u32[]{:S(2)}) async-start(s32[8,1,1]{2,1,0:T(1,128)} %copy.17), calls=%async_computation.2 | async-start | bytes 8192 | tf_op jit(solution)/shard_map/all_to_all | solution.py:35
Sparse Core Ops, SparseCore 0:
  32.0 21.5 all-gather.4
  55.8 202.0 all-gather.6
  259.9 200.4 all-gather.10
  462.4 200.1 all-gather.8
  682.9 49.5 all-reduce.2
where the time goes:
time: 765 us
  waiting for transfers between devices  655 us (86%)
  blocking collectives  43.1 us (6%)
  matrix products  31.2 us (4%)
  between operations  13.9 us (2%)
  other arithmetic  9.75 us (1%)
    all_gather x1, waiting for transfers between devices, body(): lax.all_gather(up_weight, 'fsdp', axis=0, tiled=True)  202 us
    all_gather x1, waiting for transfers between devices, body(): lax.all_gather(gate_weight, 'fsdp', axis=0, tiled=True)  200 us
    all_gather x1, waiting for transfers between devices, body(): lax.all_gather(down_weight, 'fsdp', axis=1, tiled=True)  192 us
    psum x1, waiting for transfers between devices, body(): lax.psum(partial_value.astype(jnp.bfloat16), 'tp').astype(jnp.float32)  28 us
    all_to_all x1, blocking collectives, body(): lax.all_to_all(outgoing, 'fsdp', split_axis=0, concat_axis=0, tiled=True)  21.7 us
    psum x1, blocking collectives, body(): sums, counts = lax.psum((sums, counts), 'fsdp')  21.4 us
    dot_general x1, matrix products, body(): jnp.dot(hidden, down_full, preferred_element_type=jnp.float32)  20.2 us
    all_gather x1, waiting for transfers between devices, body(): gathered = lax.all_gather(received, 'tp', axis=2, tiled=True)  19.6 us
  transfers between devices with their start and end apart: 7, of which 7 were waited for; matrix products, arithmetic and copies ran while one was open for 2% of the time, Pallas kernels for 0%

commit v1 on v0

v1 whole, which is shorter than its diff:
```python
import functools
import jax
import jax.numpy as jnp
from jax import lax
from jax.experimental import pallas as pl
from jax.experimental.pallas import tpu as pltpu
from jax.sharding import PartitionSpec as P

S = 8
epsilon = 1e-05
MESH = pl.DeviceIdType.MESH
F32 = jnp.float32
BF16 = jnp.bfloat16


def kernel(n, tp, inner, chunk, down_chunk, ahead, lag,
           packed, meta, ffn_gain, gate_w, up_w, down_w, final_gain, value_w, out,
           tok, scaled, gate_in, up_in, down_in, rs_send, rs_recv, hid, mix_send, mix_recv,
           sq_own, sq_recv, acc, stat_own, stat_recv, fin,
           tok_s, tok_r, w_s, w_r, d_s, d_r, rs_s, rs_r, h_s, h_r, m_s, m_r, q_s, q_r, st_s, st_r, f_s, f_r):
    live, width = packed.shape
    rows, units = gate_w.shape
    cols = down_w.shape[1]
    n_chunks = units // chunk
    n_down = cols // down_chunk
    f = lax.axis_index("fsdp")
    t = lax.axis_index("tp")
    o = f // inner
    i = f % inner

    def fs(outer, inn):
        return outer * inner + inn

    def remote(src, dst, ss, rs, dev):
        return pltpu.make_async_remote_copy(src_ref=src, dst_ref=dst, send_sem=ss, recv_sem=rs, device_id=dev, device_id_type=MESH)

    barrier = pltpu.get_barrier_semaphore()
    for r in range(1, n):
        pl.semaphore_signal(barrier, inc=1, device_id=((f + r) % n, t), device_id_type=MESH)
    for r in range(1, tp):
        pl.semaphore_signal(barrier, inc=1, device_id=(f, (t + r) % tp), device_id_type=MESH)
    for r in range(1, tp):
        pl.semaphore_signal(barrier, inc=1, device_id=(fs((o + r) % tp, i), o), device_id_type=MESH)

    @pl.when(o != t)
    def _():
        pl.semaphore_signal(barrier, inc=1, device_id=(f, o), device_id_type=MESH)

    diag = (o == t).astype(jnp.int32)
    pl.semaphore_wait(barrier, n - 1 + tp - 1 + tp - diag)

    def tok_copy(r):
        return remote(packed, tok.at[o], tok_s.at[r], tok_r.at[o], (fs(t, i), (t + r) % tp))

    def st_copy(r):
        return remote(stat_own, stat_recv.at[o], st_s.at[r], st_r.at[o], (fs(t, i), (t + r) % tp))

    for r in range(1, tp):
        tok_copy(r).start()

    @pl.when(o != t)
    def _():
        tok_copy(0).start()

    def w_copies(c):
        cs = pl.ds(c * chunk, chunk)
        found = []
        for r in range(1, inner):
            dev = (fs(o, (i + r) % inner), t)
            found.append(remote(gate_w.at[:, cs], gate_in.at[r - 1, :, cs], w_s.at[c, r - 1, 0], w_r.at[c, r - 1, 0], dev))
            found.append(remote(up_w.at[:, cs], up_in.at[r - 1, :, cs], w_s.at[c, r - 1, 1], w_r.at[c, r - 1, 1], dev))
        return found

    def d_copies(c):
        cs = pl.ds(c * down_chunk, down_chunk)
        return [remote(down_w.at[:, cs], down_in.at[r - 1, :, cs], d_s.at[c, r - 1], d_r.at[c, r - 1], (fs(o, (i + r) % inner), t))
                for r in range(1, inner)]

    stages = [functools.partial(w_copies, c) for c in range(n_chunks)] + [functools.partial(d_copies, c) for c in range(n_down)]

    def start_stage(k):
        if k < len(stages):
            for copy in stages[k]():
                copy.start()

    for k in range(ahead):
        start_stage(k)

    @pl.when(o == t)
    def _():
        tok[o] = packed[...]

    wide = packed[...].astype(F32)
    sq_own[...] = jnp.broadcast_to(jnp.sum(wide * wide, axis=1, keepdims=True), (live, 128))
    q_copies = [remote(sq_own, sq_recv.at[r - 1], q_s.at[r - 1], q_r.at[r - 1], (f, (t + r) % tp)) for r in range(1, tp)]
    for copy in q_copies:
        copy.start()

    mine = pl.ds(pl.multiple_of(o * width, width), width)
    gain = ffn_gain[:, mine]
    for q in range(tp):
        @pl.when((o != t) | (o != q))
        def _():
            remote(packed, tok.at[q], tok_s.at[0], tok_r.at[q], (f, t)).wait_recv()

        scaled[q * live:(q + 1) * live, :] = (tok[q].astype(F32) * gain).astype(BF16)

    for copy in q_copies:
        copy.wait_recv()
    squares = sq_own[:, :1]
    for r in range(1, tp):
        squares = squares + sq_recv[r - 1][:, :1]
    rstd = lax.rsqrt(squares / (width * tp) + epsilon)

    def rs_copies(c):
        return [remote(rs_send.at[c, (o + r) % tp], rs_recv.at[c, r - 1], rs_s.at[c, r - 1], rs_r.at[c, r - 1], (fs((o + r) % tp, i), t))
                for r in range(1, tp)]

    def h_copies(c):
        cs = pl.ds(c * chunk, chunk)
        return [remote(hid.at[o, :, cs], hid.at[o, :, cs], h_s.at[c, r - 1], h_r.at[c, r - 1], (fs((o + r) % tp, i), t))
                for r in range(1, tp)]

    def h_arrive(c):
        cs = pl.ds(c * chunk, chunk)
        for r in range(1, tp):
            src = (o - r + tp) % tp
            remote(hid.at[src, :, cs], hid.at[src, :, cs], h_s.at[c, r - 1], h_r.at[c, r - 1], (fs(src, i), t)).wait_recv()

    def x_block(r):
        k = (i - r + inner) % inner
        return scaled[:, pl.ds(pl.multiple_of(k * rows, rows), rows)]

    def finish(c):
        for copy in rs_copies(c):
            copy.wait_recv()
        both = rs_send[c, o].astype(F32)
        for r in range(1, tp):
            both = both + rs_recv[c, r - 1].astype(F32)
        both = both * rstd
        gate, up = both[:, :chunk], both[:, chunk:]
        hid[o, :, c * chunk:(c + 1) * chunk] = (gate / (1.0 + jnp.exp(-gate)) * up).astype(BF16)
        for copy in h_copies(c):
            copy.start()

    for c in range(n_chunks):
        for copy in w_copies(c):
            copy.wait_recv()
        start_stage(c + ahead)
        cs = slice(c * chunk, (c + 1) * chunk)
        for side, (own, arrived) in enumerate(((gate_w, gate_in), (up_w, up_in))):
            part = jnp.dot(x_block(0), own[:, cs], preferred_element_type=F32)
            for r in range(1, inner):
                part = part + jnp.dot(x_block(r), arrived[r - 1, :, cs], preferred_element_type=F32)
            rs_send[c, :, :, side * chunk:(side + 1) * chunk] = part.astype(BF16).reshape(tp, live, chunk)
        for copy in rs_copies(c):
            copy.start()
        if c >= lag:
            finish(c - lag)
    for c in range(n_chunks - lag, n_chunks):
        finish(c)
    for k in range(n_chunks + ahead, len(stages)):
        start_stage(k)
    for c in range(n_chunks):
        h_arrive(c)

    blocks = [(r, c) for r in range(inner) for c in range(n_down)]

    def m_copies(b):
        return [remote(mix_send.at[b, (t + r) % tp], mix_recv.at[b, r - 1], m_s.at[b, r - 1], m_r.at[b, r - 1], (f, (t + r) % tp))
                for r in range(1, tp)]

    acc[...] = jnp.zeros_like(acc)

    def mix(b):
        r, c = blocks[b]
        for copy in m_copies(b):
            copy.wait_recv()
        k = (i - r + inner) % inner
        at = pl.multiple_of(k * cols + c * down_chunk, 128)
        total = mix_send[b, t].astype(F32)
        for q in range(1, tp):
            total = total + mix_recv[b, q - 1].astype(F32)
        mixed = tok[t, :, pl.ds(at, down_chunk)].astype(F32) + total
        there = pl.ds(pl.multiple_of(o * width + at, 128), down_chunk)
        head = final_gain[:, there] * value_w[:, there]
        first, second = mixed * head, mixed * mixed
        for g in range(down_chunk // 128):
            lanes = slice(g * 128, (g + 1) * 128)
            acc[0, :live] += first[:, lanes]
            acc[1, :live] += second[:, lanes]

    for b, (r, c) in enumerate(blocks):
        cs = slice(c * down_chunk, (c + 1) * down_chunk)
        if r > 0:
            d_copies(c)[r - 1].wait_recv()
            weight = down_in[r - 1, :, cs]
        else:
            weight = down_w[:, cs]
        part = jnp.dot(hid[...].reshape(tp * live, units), weight, preferred_element_type=F32)
        mix_send[b] = part.astype(BF16).reshape(tp, live, down_chunk)
        for copy in m_copies(b):
            copy.start()
        if b >= 1:
            mix(b - 1)
    mix(len(blocks) - 1)

    ones = jnp.ones((8, 128), F32)
    for s in range(2):
        stat_own[s] = lax.dot_general(ones, acc[s], (((1,), (1,)), ((), ())), precision=lax.Precision.HIGHEST, preferred_element_type=F32)
    for r in range(1, tp):
        st_copy(r).start()

    @pl.when(o != t)
    def _():
        st_copy(0).start()

    @pl.when(o == t)
    def _():
        stat_recv[o] = stat_own[...]

    for q in range(tp):
        @pl.when((o != t) | (o != q))
        def _():
            remote(stat_own, stat_recv.at[q], st_s.at[0], st_r.at[q], (f, t)).wait_recv()

    totals = jnp.sum(stat_recv[...], axis=0)
    value = totals[0] * lax.rsqrt(totals[1] / (width * tp) + epsilon)
    begin, size, to, stratum = (meta[:, k:k + 1] for k in range(4))
    lane = lax.broadcasted_iota(jnp.int32, (n, value.shape[1]), 1)
    member = (lane >= begin) & (lane < begin + size)
    reward = jnp.sum(jnp.where(member, value[:1], 0.0), axis=1, keepdims=True) / size.astype(F32)
    lane = lax.broadcasted_iota(jnp.int32, (n, 128), 1)
    by_dest = jnp.sum(jnp.where(lane == to, reward, 0.0), axis=0, keepdims=True)
    sums = jnp.sum(jnp.where(lane == stratum, reward, 0.0), axis=0, keepdims=True)
    counts = jnp.sum(jnp.where(lane == stratum, 1.0, 0.0), axis=0, keepdims=True)
    row8 = lax.broadcasted_iota(jnp.int32, (8, 128), 0)
    lane8 = lax.broadcasted_iota(jnp.int32, (8, 128), 1)
    fin[f] = jnp.where(row8 == 0, by_dest, jnp.where(row8 == 1, sums, counts))
    f_copies = [remote(fin.at[f], fin.at[f], f_s.at[r - 1], f_r.at[r - 1], ((f + r) % n, t)) for r in range(1, n)]
    for copy in f_copies:
        copy.start()
    for r in range(1, n):
        src = (f - r + n) % n
        remote(fin.at[src], fin.at[src], f_s.at[r - 1], f_r.at[r - 1], (src, t)).wait_recv()
    grand = jnp.sum(fin[...], axis=0)
    means = grand[1:2] / jnp.where(lane8[:1] < S, grand[2:3], 1.0)
    final = jnp.where(row8 == 1, means, 0.0)
    for s in range(n):
        got = jnp.sum(jnp.where(lane8 == f, fin[s], 0.0), axis=1, keepdims=True)[:1]
        final = final + jnp.where((row8 == 0) & (lane8 == s), got, 0.0)
    out[...] = final

    for r in range(1, tp):
        tok_copy(r).wait_send()
        st_copy(r).wait_send()

    @pl.when(o != t)
    def _():
        tok_copy(0).wait_send()
        st_copy(0).wait_send()

    pending = q_copies + f_copies
    for stage in stages:
        pending += stage()
    for c in range(n_chunks):
        pending += rs_copies(c) + h_copies(c)
    for b in range(len(blocks)):
        pending += m_copies(b)
    for copy in pending:
        copy.wait_send()


def solution(mesh):
    n = mesh.shape["fsdp"]
    tp = mesh.shape["tp"]
    inner = n // tp

    def body(states, dest, lengths, strata, ffn_gain, gate_weight, up_weight, down_weight, final_gain, value_weight):
        groups, length, width = states.shape[1:]
        live = groups * length * 5 // 8
        rows, units = gate_weight.shape
        cols = down_weight.shape[1]
        chunk, down_chunk = 256, 256
        n_chunks, n_down = units // chunk, cols // down_chunk
        n_blocks = inner * n_down
        padded = -(-live // 128) * 128
        lens = lengths[0]
        slots = jnp.arange(groups, dtype=jnp.int32)
        starts = jnp.sum(jnp.where(slots[None, :] < slots[:, None], lens[None, :], 0), axis=1)
        positions = jnp.arange(length, dtype=jnp.int32)
        rank = jnp.where(positions[None, :] < lens[:, None], starts[:, None] + positions[None, :], -1).reshape(-1)
        pick = (rank[None, :] == jnp.arange(live, dtype=jnp.int32)[:, None]).astype(BF16)
        packed = jnp.dot(pick, states[0].reshape(groups * length, width), preferred_element_type=F32).astype(BF16)
        meta = jnp.stack([starts, lens, dest[0], strata[0, :, 0]], axis=1)
        vmem = pl.BlockSpec(memory_space=pltpu.VMEM)
        dma = pltpu.SemaphoreType.DMA
        out = pl.pallas_call(
            functools.partial(kernel, n, tp, inner, chunk, down_chunk, 2, 1),
            out_shape=jax.ShapeDtypeStruct((8, 128), F32),
            in_specs=[vmem] * 8,
            out_specs=vmem,
            scratch_shapes=[
                pltpu.VMEM((tp, live, width), BF16),
                pltpu.VMEM((tp * live, width), BF16),
                pltpu.VMEM((inner - 1, rows, units), BF16),
                pltpu.VMEM((inner - 1, rows, units), BF16),
                pltpu.VMEM((inner - 1, units, cols), BF16),
                pltpu.VMEM((n_chunks, tp, live, 2 * chunk), BF16),
                pltpu.VMEM((n_chunks, tp - 1, live, 2 * chunk), BF16),
                pltpu.VMEM((tp, live, units), BF16),
                pltpu.VMEM((n_blocks, tp, live, down_chunk), BF16),
                pltpu.VMEM((n_blocks, tp - 1, live, down_chunk), BF16),
                pltpu.VMEM((live, 128), F32),
                pltpu.VMEM((tp - 1, live, 128), F32),
                pltpu.VMEM((2, padded, 128), F32),
                pltpu.VMEM((2, 8, padded), F32),
                pltpu.VMEM((tp, 2, 8, padded), F32),
                pltpu.VMEM((n, 8, 128), F32),
                dma((tp,)), dma((tp,)),
                dma((n_chunks, inner - 1, 2)), dma((n_chunks, inner - 1, 2)),
                dma((n_down, inner - 1)), dma((n_down, inner - 1)),
                dma((n_chunks, tp - 1)), dma((n_chunks, tp - 1)),
                dma((n_chunks, tp - 1)), dma((n_chunks, tp - 1)),
                dma((n_blocks, tp - 1)), dma((n_blocks, tp - 1)),
                dma((tp - 1,)), dma((tp - 1,)),
                dma((tp,)), dma((tp,)),
                dma((n - 1,)), dma((n - 1,)),
            ],
            compiler_params=pltpu.CompilerParams(collective_id=0, has_side_effects=True, vmem_limit_bytes=62 << 20),
        )(packed, meta, ffn_gain[None], gate_weight, up_weight, down_weight, final_gain[None], value_weight[None])
        return out[:1, :groups], out[1, :S]

    return jax.shard_map(
        body,
        mesh=mesh,
        in_specs=(
            P("fsdp", None, None, "tp"),
            P("fsdp", None),
            P("fsdp", None),
            P("fsdp", None, None),
            P(),
            P("fsdp", "tp"),
            P("fsdp", "tp"),
            P("tp", "fsdp"),
            P(),
            P(),
        ),
        out_specs=(P("fsdp", None), P()),
        check_vma=False,
    )
```

time: 765 us -> 255 us (0.33)
  waiting for transfers between devices: 655 us -> 0 us
  Pallas kernels: 0 us -> 246 us
  blocking collectives: 43.1 us -> 0 us
  matrix products: 31.2 us -> 0.97 us
  between operations: 13.9 us -> 0.65 us
    all_gather x4 -> x0, waiting for transfers between devices: 613 us -> none  [the longest x1 202 us: body(): lax.all_gather(up_weight, 'fsdp', axis=0, tiled=True)]
    pallas_call x0 -> x1, Pallas kernels: none -> 246 us  [body(): pl.pallas_call(functools.partial(kernel, n, tp, inner, chunk, down_chunk,...]
    dot_general x2 -> x1, matrix products: 31.2 us -> 0.97 us  [body(): jnp.dot(pick, states[0].reshape(groups * length, width), preferred_elemen...]
    psum x1 -> x0, waiting for transfers between devices: 28 us -> none  [body(): lax.psum(partial_value.astype(jnp.bfloat16), 'tp').astype(jnp.float32)]
    all_to_all x1 -> x0, blocking collectives: 21.7 us -> none  [body(): lax.all_to_all(outgoing, 'fsdp', split_axis=0, concat_axis=0, tiled=True)]
    psum x1 -> x0, blocking collectives: 21.4 us -> none  [body(): sums, counts = lax.psum((sums, counts), 'fsdp')]
    all_to_all x2 -> x0, waiting for transfers between devices: 11.9 us -> none  [the longest x1 6.17 us: body(): lax.all_to_all(out_str, 'fsdp', split_axis=0, concat_axis=0, tiled=True)]
  transfers between devices with their start and end apart: 7 -> 0, of which waited for: 7 -> 0; matrix products, arithmetic and copies ran while one was open for 2% -> 0% of each run, Pallas kernels for 0% -> 0%
where the time goes in v1:
time: 255 us; the launch traced here: 254 us
  Pallas kernels  246 us (96%)
  local copies, waits for them, and re-layouts  4.67 us (2%)
    pallas_call x1, Pallas kernels, body(): pl.pallas_call(functools.partial(kernel, n, tp, inner, chunk, down_chunk,...  246 us

profile of v1, /device:TPU:0, one launch (start us, length us, event | category | flops | bytes accessed | tf_op | source)
XLA Modules:
  0.0 254.3 jit_solution(17111551348978486829)
XLA Ops:
  0.6 0.0 copy-start
  0.6 1.0 copy-done
  1.7 0.8 select_reduce_fusion
  2.4 0.1 copy.16
  2.5 0.7 add_select_fusion
  3.3 0.1 select_n.17
  3.3 0.7 copy.18
  4.1 0.7 copy.19
  4.8 0.7 copy.17
  5.5 0.7 pad_add_fusion.meta
  6.2 1.0 convolution_convert_fusion.packed
  7.2 245.8 %shard_map.113 = f32[8,128]{1,0:T(8,128)} custom-call(bf16[160,1024]{1,0:T(8,128)(2,1)} %convolution_convert_fusion.packed, s32[8,4]{1,0:T(8,128)} %pad_add_fusion.meta, f32[1,4096]{1,0:T(1,128)} %bitcast.13, bf16[512,1792]{1,0:T(8,128)(2,1)} %gate_w.1, bf16[512,1792]{1,0:T(8,128)(2,1)} %up_w.1, bf16[1792,512]{1,0:T(8,128)(2,1)} %down_w.1, ...), custom_call_target="tpu_custom_call" | custom-call | tf_op jit(solution)/shard_map/pallas_call | solution.py:298
  253.0 1.3 slice_bitcast_fusion
Async XLA Ops:
  0.6 1.0 copy-start
